TPU v7x, 32 devices: a whole 2x2x4 slice. The times are simulated.
32 devices in a mesh: groups: 2 (over x), blk: 16 (over z, y, core).
Axes of the slice: x: 2, y: 2, z: 4, core: 2. Of those that a mesh axis runs over, the one named last changes fastest.
Arguments:
- queries: bfloat16 [32, 8192], P(('groups', 'blk')), parts along dimension 0, may hold values from -100 to 100
- prefix_key_value: bfloat16 [2, 32768, 1024], P(None, ('groups', 'blk')), parts along dimension 1, may hold values from -7 to 7
- suffix_key_value: bfloat16 [32, 2, 512, 1024], P(('groups', 'blk')), parts along dimension 0, may hold values from -9 to 9
- fresh_key_value: bfloat16 [32, 2, 1024], P(('groups', 'blk')), parts along dimension 0, may hold values from -9 to 9
- lengths: int32 [32], P('groups'), parts along dimension 0, may hold values from 1 to 512, 4096 in all
- home: int32 [32], P('groups'), parts along dimension 0, may hold values from 0 to 15, each once
Outputs:
- attended: bfloat16 [32, 8192], P(('groups', 'blk')), parts along dimension 0
There are 2 independent parts, one for each index of `groups`. A program takes and returns all parts, laid end to end along the dimension named above; each array names one. Nothing has to cross between parts.
Inputs may be any that keep to these rules, and one draw needn't show every extreme that they name: Row r's suffix cache lies in slot home[r]; every slot holds exactly one row. `lengths`: some row has exactly 512 suffix tokens.
All inputs are finite; a program needn't handle non-finite values.
Results may differ from a plain program's by a relative error of at most 0.0049.
Values may be sent and summed in bfloat16 or wider, within the bound.
No kernel may reach another device: no remote copies, remote signals or barrier semaphores. Data moves between devices by JAX's collectives and lax.ppermute only.
A program may use at most 128 MiB of HBM per device.

v0:
```python
import jax
import jax.numpy as jnp
from jax import lax
from jax.sharding import PartitionSpec as P

QUERY_HEADS = 64
KEY_VALUE_HEADS = 8
HEAD_WIDTH = 128


def per_device(queries, prefix_key_value, suffix_key_value, fresh_key_value, lengths, home):
    rows_per_block = queries.shape[0]
    blocks = lax.axis_size("blk")
    my_index = lax.axis_index("blk")
    revision_count = rows_per_block * blocks
    query_group = QUERY_HEADS // KEY_VALUE_HEADS
    score_scale = HEAD_WIDTH ** (-0.5)
    prefix_length_count = prefix_key_value.shape[1]
    suffix_length_count = suffix_key_value.shape[2]
    gathered_parts = lax.all_gather(queries, "blk", axis=0, tiled=True)
    grouped_queries = gathered_parts.reshape(
        revision_count, KEY_VALUE_HEADS, query_group, HEAD_WIDTH
    )
    query_head_rows = grouped_queries.transpose(1, 0, 2, 3).reshape(
        KEY_VALUE_HEADS, revision_count * query_group, HEAD_WIDTH
    )
    key_head_rows = (
        prefix_key_value[0]
        .reshape(prefix_length_count, KEY_VALUE_HEADS, HEAD_WIDTH)
        .transpose(1, 0, 2)
    )
    value_head_rows = (
        prefix_key_value[1]
        .reshape(prefix_length_count, KEY_VALUE_HEADS, HEAD_WIDTH)
        .transpose(1, 0, 2)
    )

    def prefix_head(item):
        query_block, keys_block, values_block = item
        scores = (
            jnp.dot(query_block, keys_block.T, preferred_element_type=jnp.float32) * score_scale
        )
        peak = jnp.max(scores, axis=-1)
        exponent = jnp.exp(scores - peak[:, None])
        totals = jnp.sum(exponent, axis=-1)
        accum = jnp.dot(
            exponent.astype(jnp.bfloat16), values_block, preferred_element_type=jnp.float32
        )
        return (peak, totals, accum)

    prefix_score_peak, prefix_weight_sum, prefix_accum_sum = lax.map(
        prefix_head, (query_head_rows, key_head_rows, value_head_rows)
    )
    prefix_score_peak = prefix_score_peak.reshape(
        KEY_VALUE_HEADS, revision_count, query_group
    ).transpose(1, 0, 2)
    prefix_weight_sum = prefix_weight_sum.reshape(
        KEY_VALUE_HEADS, revision_count, query_group
    ).transpose(1, 0, 2)
    prefix_accum_sum = prefix_accum_sum.reshape(
        KEY_VALUE_HEADS, revision_count, query_group, HEAD_WIDTH
    ).transpose(1, 0, 2, 3)
    slot_ids = my_index * rows_per_block + jnp.arange(rows_per_block, dtype=jnp.int32)
    row_ids = jnp.arange(revision_count, dtype=jnp.int32)
    matches = home[None, :] == slot_ids[:, None]
    row_lookup = jnp.sum(jnp.where(matches, row_ids[None, :], 0), axis=1)
    slot_queries = grouped_queries[row_lookup]
    slot_key_rows = suffix_key_value[:, 0].reshape(
        rows_per_block, suffix_length_count, KEY_VALUE_HEADS, HEAD_WIDTH
    )
    slot_value_rows = suffix_key_value[:, 1].reshape(
        rows_per_block, suffix_length_count, KEY_VALUE_HEADS, HEAD_WIDTH
    )
    scores = (
        jnp.einsum(
            "rhgd,rthd->rhgt", slot_queries, slot_key_rows, preferred_element_type=jnp.float32
        )
        * score_scale
    )
    live_mask = (
        jnp.arange(suffix_length_count, dtype=jnp.int32)[None, :] < lengths[row_lookup][:, None]
    )
    scores = jnp.where(live_mask[:, None, None, :], scores, -jnp.inf)
    slot_score_peak = jnp.max(scores, axis=-1)
    exponent = jnp.exp(scores - slot_score_peak[..., None])
    slot_weight_sum = jnp.sum(exponent, axis=-1)
    slot_accum_sum = jnp.einsum(
        "rhgt,rthd->rhgd",
        exponent.astype(jnp.bfloat16),
        slot_value_rows,
        preferred_element_type=jnp.float32,
    )
    suffix_score_peak = (
        jnp.full((revision_count, KEY_VALUE_HEADS, query_group), -jnp.inf, jnp.float32)
        .at[row_lookup]
        .set(slot_score_peak)
    )
    suffix_weight_sum = (
        jnp.zeros((revision_count, KEY_VALUE_HEADS, query_group), jnp.float32)
        .at[row_lookup]
        .set(slot_weight_sum)
    )
    suffix_accum_sum = (
        jnp.zeros((revision_count, KEY_VALUE_HEADS, query_group, HEAD_WIDTH), jnp.float32)
        .at[row_lookup]
        .set(slot_accum_sum)
    )
    local_query_rows = queries.reshape(rows_per_block, KEY_VALUE_HEADS, query_group, HEAD_WIDTH)
    fresh_token_keys = fresh_key_value[:, 0].reshape(rows_per_block, KEY_VALUE_HEADS, HEAD_WIDTH)
    fresh_token_values = (
        fresh_key_value[:, 1]
        .reshape(rows_per_block, KEY_VALUE_HEADS, HEAD_WIDTH)
        .astype(jnp.float32)
    )
    local_score_peak = (
        jnp.einsum(
            "rhgd,rhd->rhg", local_query_rows, fresh_token_keys, preferred_element_type=jnp.float32
        )
        * score_scale
    )
    local_accum_sum = jnp.broadcast_to(
        fresh_token_values[:, :, None, :],
        (rows_per_block, KEY_VALUE_HEADS, query_group, HEAD_WIDTH),
    )
    start_offset = my_index * rows_per_block
    new_peak = lax.dynamic_update_slice_in_dim(
        jnp.full((revision_count, KEY_VALUE_HEADS, query_group), -jnp.inf, jnp.float32),
        local_score_peak,
        start_offset,
        0,
    )
    new_total = lax.dynamic_update_slice_in_dim(
        jnp.zeros((revision_count, KEY_VALUE_HEADS, query_group), jnp.float32),
        jnp.ones_like(local_score_peak),
        start_offset,
        0,
    )
    fresh_token_accum = lax.dynamic_update_slice_in_dim(
        jnp.zeros((revision_count, KEY_VALUE_HEADS, query_group, HEAD_WIDTH), jnp.float32),
        local_accum_sum,
        start_offset,
        0,
    )
    peak = jnp.maximum(prefix_score_peak, jnp.maximum(suffix_score_peak, new_peak))
    pre_fac = jnp.exp(prefix_score_peak - peak)
    suf_fac = jnp.exp(suffix_score_peak - peak)
    new_fac = jnp.exp(new_peak - peak)
    totals = pre_fac * prefix_weight_sum + suf_fac * suffix_weight_sum + new_fac * new_total
    accum = (
        pre_fac[..., None] * prefix_accum_sum
        + suf_fac[..., None] * suffix_accum_sum
        + new_fac[..., None] * fresh_token_accum
    )
    normed_half = (
        (accum / totals[..., None])
        .astype(jnp.bfloat16)
        .reshape(revision_count, QUERY_HEADS * HEAD_WIDTH)
    )
    lse = (peak + jnp.log(totals)).reshape(revision_count, QUERY_HEADS)
    landed = lax.all_to_all(
        normed_half.reshape(blocks, rows_per_block, QUERY_HEADS * HEAD_WIDTH),
        "blk",
        split_axis=0,
        concat_axis=0,
        tiled=True,
    )
    landed_lse = lax.all_to_all(
        lse.reshape(blocks, rows_per_block, QUERY_HEADS),
        "blk",
        split_axis=0,
        concat_axis=0,
        tiled=True,
    )
    highest = jnp.max(landed_lse, axis=0)
    weights = jnp.exp(landed_lse - highest[None])
    landed = landed.astype(jnp.float32).reshape(blocks, rows_per_block, QUERY_HEADS, HEAD_WIDTH)
    numerator = jnp.sum(weights[..., None] * landed, axis=0)
    denominator = jnp.sum(weights, axis=0)
    result = numerator / denominator[..., None]
    return result.reshape(rows_per_block, QUERY_HEADS * HEAD_WIDTH).astype(jnp.bfloat16)


def solution(mesh):
    placed = (
        P(("groups", "blk"), None),
        P(None, ("groups", "blk"), None),
        P(("groups", "blk"), None, None, None),
        P(("groups", "blk"), None, None),
        P("groups"),
        P("groups"),
    )
    return jax.shard_map(
        per_device,
        mesh=mesh,
        in_specs=placed,
        out_specs=P(("groups", "blk"), None),
        check_vma=False,
    )
```

profile of v0, /device:TPU:0, one launch (start us, length us, event | category | flops | bytes accessed | tf_op | source)
XLA Modules:
  0.0 108.4 jit_solution(14778481534086391625)
XLA Ops:
  0.0 1.3 %fusion.34 = s32[]{:T(128)} fusion(s32[16]{0:T(128)} %param.19, s32[]{:T(128)S(6)} %axis_index.12), kind=kLoop, calls=%fused_computation.58 | loop fusion | flops 47 | bytes 72 | tf_op jit(solution)/shard_map/reduce_sum | solution.py:66
  5.6 1.7 %fusion.40 = (bf16[1,1,512,1024]{3,2,1,0:T(8,128)(2,1)S(1)}, bf16[1,1,512,1024]{3,2,1,0:T(8,128)(2,1)S(1)}) fusion(bf16[1,2,512,1024]{3,2,1,0:T(8,128)(2,1)} %param.16), kind=kLoop, calls=%fused_computation.62 | loop fusion | bytes 4194304 | tf_op jit(solution)/shard_map/slice | solution.py:71
  8.1 24.6 %all-gather = bf16[16,1,8192]{2,1,0:T(2,128)(2,1)S(1)} all-gather(bf16[1,1,8192]{2,1,0:T(2,128)(2,1)S(1)} %bitcast.126), channel_id=1, replica_groups=mesh['groups'=2,'blk'=16] {'blk'}, dimensions={0}, use_global_device_ids=true | all-gather | bytes 278528 | tf_op jit(solution)/shard_map/all_gather | solution.py:20
  32.8 1.5 %reduce.26 = bf16[16,8192]{1,0:T(8,128)(2,1)S(1)} reduce(bf16[16,1,8192]{2,1,0:T(2,128)(2,1)S(1)} %all-gather, bf16[]{:T(256)} %constant.147), dimensions={1}, to_apply=%all-gather.reduce_sub_computation | reduce | bytes 524290 | tf_op jit(solution)/shard_map/all_gather | solution.py:20
  39.1 4.0 %fusion.39 = (bf16[1,1024,1024]{2,1,0:T(8,128)(2,1)S(1)}, bf16[1,1024,1024]{2,1,0:T(8,128)(2,1)}) fusion(bf16[2,1024,1024]{2,1,0:T(8,128)(2,1)} %param.15), kind=kLoop, calls=%fused_computation.61 | loop fusion | bytes 8388608 | tf_op jit(solution)/shard_map/slice | solution.py:33
  43.1 4.0 %copy.115 = bf16[1,1024,1024]{1,2,0:T(8,128)(2,1)} copy(bf16[1,1024,1024]{2,1,0:T(8,128)(2,1)} %get-tuple-element.164) | data formatting | bytes 4194304
  47.0 2.6 %copy.116 = bf16[1,1024,1024]{1,2,0:T(8,128)(2,1)} copy(bf16[1,1024,1024]{2,1,0:T(8,128)(2,1)S(1)} %get-tuple-element.163) | data formatting | bytes 4194304
  49.7 27.4 %while.19 = (s32[]{:T(128)}, f32[8,128]{1,0:T(8,128)S(1)}, f32[8,128]{1,0:T(8,128)S(1)}, f32[8,128,128]{2,1,0:T(8,128)}, bf16[8,128,128]{2,1,0:T(8,128)(2,1)S(1)...) while((s32[]{:T(128)}, f32[8,128]{1,0:T(8,128)S(1)}, ...), condition=%wide.region_3.4_spmd, body=%wide.region_0.3_spmd.sunk | while | flops 67895040 | bytes 2201701 | solution.py:51
  49.7 1.2 %fusion.52 = (f32[128]{0:T(128)S(1)}, f32[128,1024]{1,0:T(8,128)S(1)}) fusion(bf16[8,1024,128]{1,2,0:T(8,128)(2,1)} %get-tuple-element.241, s32[]{:T(128)} %get-tuple-element.227, bf16[8,128,128]{2,1,0:T(8,128)(2,1)S(1)} %get-tuple-element.240), kind=kOutput, calls=%fused_computation.60.clone.1 | convolution fusion | flops 33816448 | bytes 820736 | tf_op jit(solution)/shard_map/while/body/eval_jaxpr/dot_general | solution.py:41
  51.0 1.9 %fusion.54 = f32[8,128,128]{2,1,0:T(8,128)} fusion(f32[8,128,128]{2,1,0:T(8,128)} %get-tuple-element.230, s32[]{:T(128)} %get-tuple-element.227, f32[128,1024]{1,0:T(8,128)S(1)} %get-tuple-element.217, bf16[8,1024,128]{1,2,0:T(8,128)(2,1)} %get-tuple-element.242, f32[128]{0:T(128)S(1)} %get-tuple-element.216), kind=kOutput, calls=%fused_computation.2.clone.1 | convolution fusion | flops 33816576 | bytes 853504 | tf_op jit(solution)/shard_map/while/body/eval_jaxpr/dot_general | solution.py:46
  53.2 1.2 %fusion.52 = (f32[128]{0:T(128)S(1)}, f32[128,1024]{1,0:T(8,128)S(1)}) fusion(bf16[8,1024,128]{1,2,0:T(8,128)(2,1)} %get-tuple-element.241, s32[]{:T(128)} %get-tuple-element.227, bf16[8,128,128]{2,1,0:T(8,128)(2,1)S(1)} %get-tuple-element.240), kind=kOutput, calls=%fused_computation.60.clone.1 | convolution fusion | flops 33816448 | bytes 820736 | tf_op jit(solution)/shard_map/while/body/eval_jaxpr/dot_general | solution.py:41
  54.4 1.9 %fusion.54 = f32[8,128,128]{2,1,0:T(8,128)} fusion(f32[8,128,128]{2,1,0:T(8,128)} %get-tuple-element.230, s32[]{:T(128)} %get-tuple-element.227, f32[128,1024]{1,0:T(8,128)S(1)} %get-tuple-element.217, bf16[8,1024,128]{1,2,0:T(8,128)(2,1)} %get-tuple-element.242, f32[128]{0:T(128)S(1)} %get-tuple-element.216), kind=kOutput, calls=%fused_computation.2.clone.1 | convolution fusion | flops 33816576 | bytes 853504 | tf_op jit(solution)/shard_map/while/body/eval_jaxpr/dot_general | solution.py:46
  57.8 1.9 %fusion.54 = f32[8,128,128]{2,1,0:T(8,128)} fusion(f32[8,128,128]{2,1,0:T(8,128)} %get-tuple-element.230, s32[]{:T(128)} %get-tuple-element.227, f32[128,1024]{1,0:T(8,128)S(1)} %get-tuple-element.217, bf16[8,1024,128]{1,2,0:T(8,128)(2,1)} %get-tuple-element.242, f32[128]{0:T(128)S(1)} %get-tuple-element.216), kind=kOutput, calls=%fused_computation.2.clone.1 | convolution fusion | flops 33816576 | bytes 853504 | tf_op jit(solution)/shard_map/while/body/eval_jaxpr/dot_general | solution.py:46
  60.0 1.2 %fusion.52 = (f32[128]{0:T(128)S(1)}, f32[128,1024]{1,0:T(8,128)S(1)}) fusion(bf16[8,1024,128]{1,2,0:T(8,128)(2,1)} %get-tuple-element.241, s32[]{:T(128)} %get-tuple-element.227, bf16[8,128,128]{2,1,0:T(8,128)(2,1)S(1)} %get-tuple-element.240), kind=kOutput, calls=%fused_computation.60.clone.1 | convolution fusion | flops 33816448 | bytes 820736 | tf_op jit(solution)/shard_map/while/body/eval_jaxpr/dot_general | solution.py:41
  61.3 1.9 %fusion.54 = f32[8,128,128]{2,1,0:T(8,128)} fusion(f32[8,128,128]{2,1,0:T(8,128)} %get-tuple-element.230, s32[]{:T(128)} %get-tuple-element.227, f32[128,1024]{1,0:T(8,128)S(1)} %get-tuple-element.217, bf16[8,1024,128]{1,2,0:T(8,128)(2,1)} %get-tuple-element.242, f32[128]{0:T(128)S(1)} %get-tuple-element.216), kind=kOutput, calls=%fused_computation.2.clone.1 | convolution fusion | flops 33816576 | bytes 853504 | tf_op jit(solution)/shard_map/while/body/eval_jaxpr/dot_general | solution.py:46
  63.4 1.2 %fusion.52 = (f32[128]{0:T(128)S(1)}, f32[128,1024]{1,0:T(8,128)S(1)}) fusion(bf16[8,1024,128]{1,2,0:T(8,128)(2,1)} %get-tuple-element.241, s32[]{:T(128)} %get-tuple-element.227, bf16[8,128,128]{2,1,0:T(8,128)(2,1)S(1)} %get-tuple-element.240), kind=kOutput, calls=%fused_computation.60.clone.1 | convolution fusion | flops 33816448 | bytes 820736 | tf_op jit(solution)/shard_map/while/body/eval_jaxpr/dot_general | solution.py:41
  64.7 1.9 %fusion.54 = f32[8,128,128]{2,1,0:T(8,128)} fusion(f32[8,128,128]{2,1,0:T(8,128)} %get-tuple-element.230, s32[]{:T(128)} %get-tuple-element.227, f32[128,1024]{1,0:T(8,128)S(1)} %get-tuple-element.217, bf16[8,1024,128]{1,2,0:T(8,128)(2,1)} %get-tuple-element.242, f32[128]{0:T(128)S(1)} %get-tuple-element.216), kind=kOutput, calls=%fused_computation.2.clone.1 | convolution fusion | flops 33816576 | bytes 853504 | tf_op jit(solution)/shard_map/while/body/eval_jaxpr/dot_general | solution.py:46
  68.1 1.9 %fusion.54 = f32[8,128,128]{2,1,0:T(8,128)} fusion(f32[8,128,128]{2,1,0:T(8,128)} %get-tuple-element.230, s32[]{:T(128)} %get-tuple-element.227, f32[128,1024]{1,0:T(8,128)S(1)} %get-tuple-element.217, bf16[8,1024,128]{1,2,0:T(8,128)(2,1)} %get-tuple-element.242, f32[128]{0:T(128)S(1)} %get-tuple-element.216), kind=kOutput, calls=%fused_computation.2.clone.1 | convolution fusion | flops 33816576 | bytes 853504 | tf_op jit(solution)/shard_map/while/body/eval_jaxpr/dot_general | solution.py:46
  71.5 1.9 %fusion.54 = f32[8,128,128]{2,1,0:T(8,128)} fusion(f32[8,128,128]{2,1,0:T(8,128)} %get-tuple-element.230, s32[]{:T(128)} %get-tuple-element.227, f32[128,1024]{1,0:T(8,128)S(1)} %get-tuple-element.217, bf16[8,1024,128]{1,2,0:T(8,128)(2,1)} %get-tuple-element.242, f32[128]{0:T(128)S(1)} %get-tuple-element.216), kind=kOutput, calls=%fused_computation.2.clone.1 | convolution fusion | flops 33816576 | bytes 853504 | tf_op jit(solution)/shard_map/while/body/eval_jaxpr/dot_general | solution.py:46
  75.0 1.9 %fusion.54 = f32[8,128,128]{2,1,0:T(8,128)} fusion(f32[8,128,128]{2,1,0:T(8,128)} %get-tuple-element.230, s32[]{:T(128)} %get-tuple-element.227, f32[128,1024]{1,0:T(8,128)S(1)} %get-tuple-element.217, bf16[8,1024,128]{1,2,0:T(8,128)(2,1)} %get-tuple-element.242, f32[128]{0:T(128)S(1)} %get-tuple-element.216), kind=kOutput, calls=%fused_computation.2.clone.1 | convolution fusion | flops 33816576 | bytes 853504 | tf_op jit(solution)/shard_map/while/body/eval_jaxpr/dot_general | solution.py:46
  79.7 3.5 %all-to-all-start = ((f32[16,1,64]{2,1,0:T(1,128)}), f32[16,1,64]{2,1,0:T(1,128)S(1)}, u32[]{:S(2)}, u32[]{:S(2)}) async-start(f32[16,1,64]{2,1,0:T(1,128)} %copy.100), calls=%async_computation | async-start | bytes 16384 | tf_op jit(solution)/shard_map/all_to_all | solution.py:167
  87.3 2.2 %reduce.30 = bf16[16,8192]{1,0:T(8,128)(2,1)S(1)} reduce(bf16[16,1,8192]{2,1,0:T(2,128)(2,1)S(1)} %reshape_reshape.8, bf16[]{:T(256)} %broadcast.203), dimensions={1}, to_apply=%reshape_reshape.8.reduce_sub_computation | reduce | bytes 524290 | tf_op jit(solution)/shard_map/reshape;reshape | solution.py:161
  90.4 6.0 %all-to-all-start.1 = ((bf16[16,2,4096]{2,1,0:T(2,128)(2,1)}), bf16[16,2,4096]{2,1,0:T(2,128)(2,1)S(1)}, u32[]{:S(2)}, u32[]{:S(2)}) async-start(bf16[16,2,4096]{2,1,0:T(2,128)(2,1)} %reshape.327), calls=%async_computation.1 | async-start | bytes 524288 | tf_op jit(solution)/shard_map/all_to_all | solution.py:160
  96.5 9.9 %all-to-all-done.1 = bf16[16,2,4096]{2,1,0:T(2,128)(2,1)S(1)} async-done(((bf16[16,2,4096]{2,1,0:T(2,128)(2,1)}), bf16[16,2,4096]{2,1,0:T(2,128)(2,1)S(1)}, u32[]{:S(2)}, u32[]{:S(2)}) %all-to-all-start.1) | async-done | bytes 262176 | tf_op jit(solution)/shard_map/all_to_all | solution.py:160
  (100 shorter events, 24.9 us)
Async XLA Ops:
  7.3 0.8 copy-start.1
  7.3 27.0 %copy-start.7 = (s32[3]{0:T(128)S(1)}, s32[3]{0:T(128)}, u32[]{:S(2)}) copy-start(s32[3]{0:T(128)} %constant.101.clone.1) | copy-start | bytes 40
  7.9 30.4 %copy-start.5 = (bf16[1,2,1024]{2,1,0:T(2,128)(2,1)S(1)}, bf16[1,2,1024]{2,1,0:T(2,128)(2,1)}, u32[]{:S(2)}) copy-start(bf16[1,2,1024]{2,1,0:T(2,128)(2,1)} %param.17) | copy-start | bytes 12292
  49.7 27.8 %copy-start.4 = (f32[1,8,8]{0,2,1:T(8,128)S(1)}, f32[1,8,8]{0,2,1:T(8,128)}, u32[]{:S(2)}) copy-start(f32[1,8,8]{0,2,1:T(8,128)} %copy.96) | copy-start | bytes 772
  49.7 28.5 %copy-start.2 = (f32[1,8,8]{0,2,1:T(8,128)S(1)}, f32[1,8,8]{0,2,1:T(8,128)}, u32[]{:S(2)}) copy-start(f32[1,8,8]{0,2,1:T(8,128)} %copy.99) | copy-start | bytes 772
  49.7 29.1 %copy-start.3 = (f32[1,8,8]{0,2,1:T(8,128)S(1)}, f32[1,8,8]{0,2,1:T(8,128)}, u32[]{:S(2)}) copy-start(f32[1,8,8]{0,2,1:T(8,128)} %copy.97) | copy-start | bytes 772
  49.7 33.9 %copy-start.6 = (s32[4]{0:T(128)S(1)}, s32[4]{0:T(128)}, u32[]{:S(2)}) copy-start(s32[4]{0:T(128)} %constant.106.clone.1) | copy-start | bytes 52
  79.7 10.7 %all-to-all-start = ((f32[16,1,64]{2,1,0:T(1,128)}), f32[16,1,64]{2,1,0:T(1,128)S(1)}, u32[]{:S(2)}, u32[]{:S(2)}) async-start(f32[16,1,64]{2,1,0:T(1,128)} %copy.100), calls=%async_computation | async-start | bytes 16384 | tf_op jit(solution)/shard_map/all_to_all | solution.py:167
  84.3 1.6 %copy-start = (f32[8,128,128]{2,1,0:T(8,128)S(1)}, f32[8,128,128]{2,1,0:T(8,128)}, u32[]{:S(2)}) copy-start(f32[8,128,128]{2,1,0:T(8,128)} %get-tuple-element.82) | copy-start | bytes 1572868
  90.4 16.0 %all-to-all-start.1 = ((bf16[16,2,4096]{2,1,0:T(2,128)(2,1)}), bf16[16,2,4096]{2,1,0:T(2,128)(2,1)S(1)}, u32[]{:S(2)}, u32[]{:S(2)}) async-start(bf16[16,2,4096]{2,1,0:T(2,128)(2,1)} %reshape.327), calls=%async_computation.1 | async-start | bytes 524288 | tf_op jit(solution)/shard_map/all_to_all | solution.py:160
where the time goes:
time: 109 us; the launch traced here: 108 us
  matrix products  26.9 us (25%)
  blocking collectives  24.6 us (23%)
  local copies, waits for them, and re-layouts  22.6 us (21%)
  other arithmetic  12.5 us (11%)
  waiting for transfers between devices  9.93 us (9%)
  starting transfers between devices  9.44 us (9%)
  between operations  2.32 us (2%)
    all_gather x1, blocking collectives, per_device(): gathered_parts = lax.all_gather(queries, 'blk', axis=0, tiled=True)  24.6 us
    dot_general x8, matrix products, prefix_head(): jnp.dot(exponent.astype(jnp.bfloat16), values_block, preferred_element_ty...  14.9 us
    dot_general x8, matrix products, prefix_head(): jnp.dot(query_block, keys_block.T, preferred_element_type=jnp.float32)  9.99 us
    all_to_all x1, waiting for transfers between devices, per_device(): lax.all_to_all(normed_half.reshape(blocks, rows_per_block, QUERY_HEADS *...  9.93 us
    unnamed x23, local copies, waits for them, and re-layouts  9.02 us
    all_to_all x1, starting transfers between devices, per_device(): lax.all_to_all(normed_half.reshape(blocks, rows_per_block, QUERY_HEADS *...  5.97 us
    slice x1, local copies, waits for them, and re-layouts, per_device(): prefix_key_value[1]  3.96 us
    all_to_all x1, starting transfers between devices, per_device(): lax.all_to_all(lse.reshape(blocks, rows_per_block, QUERY_HEADS), 'blk', s...  3.47 us
  transfers between devices with their start and end apart: 2, of which 1 were waited for; matrix products, arithmetic and copies ran while one was open for 7% of the time, Pallas kernels for 0%

commit v1 on v0

--- a/solution.py
+++ b/solution.py
@@ -6,6 +6,24 @@
 QUERY_HEADS = 64
 KEY_VALUE_HEADS = 8
 HEAD_WIDTH = 128
+
+
+def joined_along(blocks, dim):
+    blocks = jnp.moveaxis(blocks, 0, dim)
+    lengths = blocks.shape
+    return blocks.reshape(*lengths[:dim], lengths[dim] * lengths[dim + 1], *lengths[dim + 2 :])
+
+
+def grow_blocks(array, axis):
+    size = lax.axis_size(axis)
+    parts = array[None]
+    for level in range(size.bit_length() - 1):
+        apart = 1 << level
+        received = lax.ppermute(parts, axis, [(i, i ^ apart) for i in range(size)])
+        both = jnp.stack([parts, received])
+        upper = lax.axis_index(axis) >> level & 1
+        parts = jnp.where(upper == 0, both, both[::-1]).reshape(-1, *array.shape)
+    return parts
 
 
 def per_device(queries, prefix_key_value, suffix_key_value, fresh_key_value, lengths, home):
@@ -17,7 +35,7 @@
     score_scale = HEAD_WIDTH ** (-0.5)
     prefix_length_count = prefix_key_value.shape[1]
     suffix_length_count = suffix_key_value.shape[2]
-    gathered_parts = lax.all_gather(queries, "blk", axis=0, tiled=True)
+    gathered_parts = joined_along(grow_blocks(queries, "blk"), 0)
     grouped_queries = gathered_parts.reshape(
         revision_count, KEY_VALUE_HEADS, query_group, HEAD_WIDTH
     )

time: 109 us -> 94.9 us (0.87)
  blocking collectives: 24.6 us -> 0 us
  starting transfers between devices: 9.44 us -> 17.4 us
  waiting for transfers between devices: 9.93 us -> 11.9 us
  local copies, waits for them, and re-layouts: 22.6 us -> 24.3 us
    all_gather x1 -> x0, blocking collectives: 24.6 us -> none  [per_device(): gathered_parts = lax.all_gather(queries, 'blk', axis=0, tiled=True)]
    ppermute x0 -> x4, starting transfers between devices: none -> 7.36 us  [grow_blocks(): received = lax.ppermute(parts, axis, [(i, i ^ apart) for i in range(size)])]
    slice x1, local copies, waits for them, and re-layouts: 3.96 us -> 1.74 us  [per_device(): prefix_key_value[1]]
    ppermute x0 -> x4, waiting for transfers between devices: none -> 1.93 us  [grow_blocks(): received = lax.ppermute(parts, axis, [(i, i ^ apart) for i in range(size)])]
    unnamed x23, local copies, waits for them, and re-layouts: 9.02 us -> 10.8 us
    rev x0 -> x1, local copies, waits for them, and re-layouts: none -> 1.65 us  [grow_blocks(): parts = jnp.where(upper == 0, both, both[::-1]).reshape(-1, *array.shape)]
    all_gather x1 -> x0, other arithmetic: 1.52 us -> none  [per_device(): gathered_parts = lax.all_gather(queries, 'blk', axis=0, tiled=True)]
    slice x1, local copies, waits for them, and re-layouts: 1.71 us -> 3.17 us  [per_device(): suffix_key_value[:, 1]]
  transfers between devices with their start and end apart: 2 -> 6, of which waited for: 1 -> 2; matrix products, arithmetic and copies ran while one was open for 7% -> 28% of each run, Pallas kernels for 0% -> 0%
where the time goes in v1:
time: 94.9 us; the launch traced here: 94 us
  matrix products  26.4 us (28%)
  local copies, waits for them, and re-layouts  24.3 us (26%)
  starting transfers between devices  17.4 us (18%)
  waiting for transfers between devices  11.9 us (13%)
  other arithmetic  11.5 us (12%)
  between operations  2.38 us (3%)
    dot_general x8, matrix products, prefix_head(): jnp.dot(exponent.astype(jnp.bfloat16), values_block, preferred_element_ty...  14.9 us
    unnamed x23, local copies, waits for them, and re-layouts  10.8 us
    dot_general x8, matrix products, prefix_head(): jnp.dot(query_block, keys_block.T, preferred_element_type=jnp.float32)  9.99 us
    all_to_all x1, waiting for transfers between devices, per_device(): lax.all_to_all(normed_half.reshape(blocks, rows_per_block, QUERY_HEADS *...  9.93 us
    ppermute x4, starting transfers between devices, grow_blocks(): received = lax.ppermute(parts, axis, [(i, i ^ apart) for i in range(size)])  7.36 us
    all_to_all x1, starting transfers between devices, per_device(): lax.all_to_all(normed_half.reshape(blocks, rows_per_block, QUERY_HEADS *...  6.01 us
    all_to_all x1, starting transfers between devices, per_device(): lax.all_to_all(lse.reshape(blocks, rows_per_block, QUERY_HEADS), 'blk', s...  4.02 us
    slice x1, local copies, waits for them, and re-layouts, per_device(): suffix_key_value[:, 1]  3.17 us
  transfers between devices with their start and end apart: 6, of which 2 were waited for; matrix products, arithmetic and copies ran while one was open for 28% of the time, Pallas kernels for 0%

profile of v1, /device:TPU:0, one launch (start us, length us, event | category | flops | bytes accessed | tf_op | source)
XLA Modules:
  0.0 94.0 jit_solution(9359751645434789923)
XLA Ops:
  0.5 3.2 %fusion.43 = (bf16[1,1,512,1024]{3,2,1,0:T(8,128)(2,1)}, bf16[1,1,512,1024]{3,2,1,0:T(8,128)(2,1)}) fusion(bf16[1,2,512,1024]{3,2,1,0:T(8,128)(2,1)} %param.16), kind=kLoop, calls=%fused_computation.73 | loop fusion | bytes 4194304 | tf_op jit(solution)/shard_map/slice | solution.py:89
  3.7 1.7 %fusion.42 = (bf16[1,1024,1024]{2,1,0:T(8,128)(2,1)S(1)}, bf16[1,1024,1024]{2,1,0:T(8,128)(2,1)}) fusion(bf16[2,1024,1024]{2,1,0:T(8,128)(2,1)S(1)} %copy-done), kind=kLoop, calls=%fused_computation.72 | loop fusion | bytes 8388608 | tf_op jit(solution)/shard_map/slice | solution.py:51
  7.3 1.7 %rev.12 = bf16[2,1,1,8192]{3,0,2,1:T(2,128)(2,1)S(1)} reverse(bf16[2,1,1,8192]{3,0,2,1:T(2,128)(2,1)S(1)} %pad_maximum_fusion.3), dimensions={0} | reverse | bytes 65536 | tf_op jit(solution)/shard_map/rev | solution.py:25
  9.0 2.6 %collective-permute-start.1 = (bf16[2,1,8192]{2,0,1:T(2,128)(2,1)S(1)}, bf16[2,1,8192]{2,0,1:T(2,128)(2,1)S(1)}, u32[]{:S(2)}, u32[]{:S(2)}) collective-permute-start(bf16[2,1,8192]{2,0,1:T(2,128)(2,1)S(1)} %get-tuple-element.161), channel_id=1, source_target_pairs={{0,2},{1,3},{2,0},{3,1},{4,6},{5,7},{6,4},{7,5},{8,10},{9,11},{10,... | collective-permute-start | bytes 98312 | tf_op jit(solution)/shard_map/ppermute | solution.py:22
  15.0 1.6 %collective-permute-start.2 = (bf16[4,1,8192]{2,0,1:T(4,128)(2,1)S(1)}, bf16[4,1,8192]{2,0,1:T(4,128)(2,1)S(1)}, u32[]{:S(2)}, u32[]{:S(2)}) collective-permute-start(bf16[4,1,8192]{2,0,1:T(4,128)(2,1)S(1)} %reshape.267), channel_id=1, source_target_pairs={{0,4},{1,5},{2,6},{3,7},{4,0},{5,1},{6,2},{7,3},{8,12},{9,13},{10,... | collective-permute-start | bytes 196616 | tf_op jit(solution)/shard_map/ppermute | solution.py:22
  17.4 1.9 %collective-permute-done.2 = bf16[4,1,8192]{2,0,1:T(4,128)(2,1)S(1)} collective-permute-done((bf16[4,1,8192]{2,0,1:T(4,128)(2,1)S(1)}, bf16[4,1,8192]{2,0,1:T(4,128)(2,1)S(1)}, u32[]{:S(2)}, u32[]{:S(2)}) %collective-permute-start.2) | collective-permute-done | bytes 65568 | tf_op jit(solution)/shard_map/ppermute | solution.py:22
  19.5 2.7 %collective-permute-start.3 = (bf16[8,1,8192]{2,0,1:T(8,128)(2,1)S(1)}, bf16[8,1,8192]{2,0,1:T(8,128)(2,1)S(1)}, u32[]{:S(2)}, u32[]{:S(2)}) collective-permute-start(bf16[8,1,8192]{2,0,1:T(8,128)(2,1)S(1)} %reshape.268), channel_id=1, source_target_pairs={{0,8},{1,9},{2,10},{3,11},{4,12},{5,13},{6,14},{7,15},{8,0},{9,1},... | collective-permute-start | bytes 393224 | tf_op jit(solution)/shard_map/ppermute | solution.py:22
  22.8 1.5 %copy.103 = bf16[1,1,512,1024]{2,3,1,0:T(8,128)(2,1)S(1)} copy(bf16[1,1,512,1024]{3,2,1,0:T(8,128)(2,1)} %get-tuple-element.159) | data formatting | bytes 2097152
  24.4 4.0 %copy.101 = bf16[1,1024,1024]{1,2,0:T(8,128)(2,1)} copy(bf16[1,1024,1024]{2,1,0:T(8,128)(2,1)} %get-tuple-element.157) | data formatting | bytes 4194304
  28.3 2.6 %copy.102 = bf16[1,1024,1024]{1,2,0:T(8,128)(2,1)} copy(bf16[1,1024,1024]{2,1,0:T(8,128)(2,1)S(1)} %get-tuple-element.156) | data formatting | bytes 4194304
  35.1 27.4 %while.19 = (s32[]{:T(128)}, f32[8,128]{1,0:T(8,128)S(1)}, f32[8,128]{1,0:T(8,128)S(1)}, f32[8,128,128]{2,1,0:T(8,128)}, bf16[8,128,128]{2,1,0:T(8,128)(2,1)S(1)...) while((s32[]{:T(128)}, f32[8,128]{1,0:T(8,128)S(1)}, ...), condition=%wide.region_3.4_spmd, body=%wide.region_0.3_spmd.sunk | while | flops 67895040 | bytes 2201701 | solution.py:69
  36.4 1.9 %fusion.57 = f32[8,128,128]{2,1,0:T(8,128)} fusion(f32[8,128,128]{2,1,0:T(8,128)} %get-tuple-element.225, s32[]{:T(128)} %get-tuple-element.222, f32[128,1024]{1,0:T(8,128)S(1)} %get-tuple-element.212, bf16[8,1024,128]{1,2,0:T(8,128)(2,1)} %get-tuple-element.237, f32[128]{0:T(128)S(1)} %get-tuple-element.211), kind=kOutput, calls=%fused_computation.2.clone.1 | convolution fusion | flops 33816576 | bytes 853504 | tf_op jit(solution)/shard_map/while/body/eval_jaxpr/dot_general | solution.py:64
  39.8 1.9 %fusion.57 = f32[8,128,128]{2,1,0:T(8,128)} fusion(f32[8,128,128]{2,1,0:T(8,128)} %get-tuple-element.225, s32[]{:T(128)} %get-tuple-element.222, f32[128,1024]{1,0:T(8,128)S(1)} %get-tuple-element.212, bf16[8,1024,128]{1,2,0:T(8,128)(2,1)} %get-tuple-element.237, f32[128]{0:T(128)S(1)} %get-tuple-element.211), kind=kOutput, calls=%fused_computation.2.clone.1 | convolution fusion | flops 33816576 | bytes 853504 | tf_op jit(solution)/shard_map/while/body/eval_jaxpr/dot_general | solution.py:64
  43.3 1.9 %fusion.57 = f32[8,128,128]{2,1,0:T(8,128)} fusion(f32[8,128,128]{2,1,0:T(8,128)} %get-tuple-element.225, s32[]{:T(128)} %get-tuple-element.222, f32[128,1024]{1,0:T(8,128)S(1)} %get-tuple-element.212, bf16[8,1024,128]{1,2,0:T(8,128)(2,1)} %get-tuple-element.237, f32[128]{0:T(128)S(1)} %get-tuple-element.211), kind=kOutput, calls=%fused_computation.2.clone.1 | convolution fusion | flops 33816576 | bytes 853504 | tf_op jit(solution)/shard_map/while/body/eval_jaxpr/dot_general | solution.py:64
  46.7 1.9 %fusion.57 = f32[8,128,128]{2,1,0:T(8,128)} fusion(f32[8,128,128]{2,1,0:T(8,128)} %get-tuple-element.225, s32[]{:T(128)} %get-tuple-element.222, f32[128,1024]{1,0:T(8,128)S(1)} %get-tuple-element.212, bf16[8,1024,128]{1,2,0:T(8,128)(2,1)} %get-tuple-element.237, f32[128]{0:T(128)S(1)} %get-tuple-element.211), kind=kOutput, calls=%fused_computation.2.clone.1 | convolution fusion | flops 33816576 | bytes 853504 | tf_op jit(solution)/shard_map/while/body/eval_jaxpr/dot_general | solution.py:64
  50.1 1.9 %fusion.57 = f32[8,128,128]{2,1,0:T(8,128)} fusion(f32[8,128,128]{2,1,0:T(8,128)} %get-tuple-element.225, s32[]{:T(128)} %get-tuple-element.222, f32[128,1024]{1,0:T(8,128)S(1)} %get-tuple-element.212, bf16[8,1024,128]{1,2,0:T(8,128)(2,1)} %get-tuple-element.237, f32[128]{0:T(128)S(1)} %get-tuple-element.211), kind=kOutput, calls=%fused_computation.2.clone.1 | convolution fusion | flops 33816576 | bytes 853504 | tf_op jit(solution)/shard_map/while/body/eval_jaxpr/dot_general | solution.py:64
  53.5 1.9 %fusion.57 = f32[8,128,128]{2,1,0:T(8,128)} fusion(f32[8,128,128]{2,1,0:T(8,128)} %get-tuple-element.225, s32[]{:T(128)} %get-tuple-element.222, f32[128,1024]{1,0:T(8,128)S(1)} %get-tuple-element.212, bf16[8,1024,128]{1,2,0:T(8,128)(2,1)} %get-tuple-element.237, f32[128]{0:T(128)S(1)} %get-tuple-element.211), kind=kOutput, calls=%fused_computation.2.clone.1 | convolution fusion | flops 33816576 | bytes 853504 | tf_op jit(solution)/shard_map/while/body/eval_jaxpr/dot_general | solution.py:64
  57.0 1.9 %fusion.57 = f32[8,128,128]{2,1,0:T(8,128)} fusion(f32[8,128,128]{2,1,0:T(8,128)} %get-tuple-element.225, s32[]{:T(128)} %get-tuple-element.222, f32[128,1024]{1,0:T(8,128)S(1)} %get-tuple-element.212, bf16[8,1024,128]{1,2,0:T(8,128)(2,1)} %get-tuple-element.237, f32[128]{0:T(128)S(1)} %get-tuple-element.211), kind=kOutput, calls=%fused_computation.2.clone.1 | convolution fusion | flops 33816576 | bytes 853504 | tf_op jit(solution)/shard_map/while/body/eval_jaxpr/dot_general | solution.py:64
  60.4 1.9 %fusion.57 = f32[8,128,128]{2,1,0:T(8,128)} fusion(f32[8,128,128]{2,1,0:T(8,128)} %get-tuple-element.225, s32[]{:T(128)} %get-tuple-element.222, f32[128,1024]{1,0:T(8,128)S(1)} %get-tuple-element.212, bf16[8,1024,128]{1,2,0:T(8,128)(2,1)} %get-tuple-element.237, f32[128]{0:T(128)S(1)} %get-tuple-element.211), kind=kOutput, calls=%fused_computation.2.clone.1 | convolution fusion | flops 33816576 | bytes 853504 | tf_op jit(solution)/shard_map/while/body/eval_jaxpr/dot_general | solution.py:64
  65.3 4.0 %all-to-all-start = ((f32[16,1,64]{2,1,0:T(1,128)}), f32[16,1,64]{2,1,0:T(1,128)S(1)}, u32[]{:S(2)}, u32[]{:S(2)}) async-start(f32[16,1,64]{2,1,0:T(1,128)} %copy.86), calls=%async_computation | async-start | bytes 16384 | tf_op jit(solution)/shard_map/all_to_all | solution.py:185
  70.4 1.7 %fusion.19 = bf16[16,8,8,128]{3,2,1,0:T(8,128)(2,1)S(1)} fusion(f32[16,8,8,128]{3,2,1,0:T(8,128)} %broadcast_dynamic-update-slice_fusion, f32[16,8,8,128]{3,2,1,0:T(8,128)S(1)} %fusion.15, f32[16,8,8]{2,1,0:T(8,128)S(1)} %copy.93, f32[16,8,8]{2,1,0:T(8,128)S(1)} %copy.92, f32[16,8,8]{2,1,0:T(8,128)S(1)} %copy.89, f32[16,8,8]{2,1,0:T(8,128)S(1)} %copy.87, ...), kind=kLoop, calls=%fused_computation.25 | loop fusion | flops 917504 | bytes 1851392 | tf_op jit(solution)/shard_map/convert_element_type | solution.py:174
  72.8 2.2 %reduce.29 = bf16[16,8192]{1,0:T(8,128)(2,1)S(1)} reduce(bf16[16,1,8192]{2,1,0:T(2,128)(2,1)S(1)} %reshape_reshape.8, bf16[]{:T(256)} %broadcast.202), dimensions={1}, to_apply=%reshape_reshape.8.reduce_sub_computation | reduce | bytes 524290 | tf_op jit(solution)/shard_map/reshape;reshape | solution.py:179
  75.9 6.0 %all-to-all-start.1 = ((bf16[16,2,4096]{2,1,0:T(2,128)(2,1)}), bf16[16,2,4096]{2,1,0:T(2,128)(2,1)S(1)}, u32[]{:S(2)}, u32[]{:S(2)}) async-start(bf16[16,2,4096]{2,1,0:T(2,128)(2,1)} %reshape.331), calls=%async_computation.1 | async-start | bytes 524288 | tf_op jit(solution)/shard_map/all_to_all | solution.py:178
  82.0 9.9 %all-to-all-done.1 = bf16[16,2,4096]{2,1,0:T(2,128)(2,1)S(1)} async-done(((bf16[16,2,4096]{2,1,0:T(2,128)(2,1)}), bf16[16,2,4096]{2,1,0:T(2,128)(2,1)S(1)}, u32[]{:S(2)}, u32[]{:S(2)}) %all-to-all-start.1) | async-done | bytes 262176 | tf_op jit(solution)/shard_map/all_to_all | solution.py:178
  (119 shorter events, 29.3 us)
Async XLA Ops:
  0.0 7.2 %collective-permute-start = (bf16[1,1,8192]{2,1,0:T(2,128)(2,1)}, bf16[1,1,8192]{2,1,0:T(2,128)(2,1)S(1)}, u32[]{:S(2)}, u32[]{:S(2)}) collective-permute-start(bf16[1,1,8192]{2,1,0:T(2,128)(2,1)} %bitcast.146), channel_id=1, source_target_pairs={{0,1},{1,0},{2,3},{3,2},{4,5},{5,4},{6,7},{7,6},{8,9},{9,8},{10,11... | collective-permute-start | bytes 49160 | tf_op jit(solution)/shard_map/ppermute | solution.py:22
  0.5 3.2 %copy-start = (bf16[2,1024,1024]{2,1,0:T(8,128)(2,1)S(1)}, bf16[2,1024,1024]{2,1,0:T(8,128)(2,1)}, u32[]{:S(2)}) copy-start(bf16[2,1024,1024]{2,1,0:T(8,128)(2,1)} %param.15) | copy-start | bytes 12582916
  3.7 1.8 %copy-start.2 = (bf16[1,8192]{1,0:T(2,128)(2,1)S(1)}, bf16[1,8192]{1,0:T(2,128)(2,1)}, u32[]{:S(2)}) copy-start(bf16[1,8192]{1,0:T(2,128)(2,1)} %param.14) | copy-start | bytes 49156
  3.7 1.9 %copy-start.3 = (bf16[1,2,1024]{2,1,0:T(2,128)(2,1)S(1)}, bf16[1,2,1024]{2,1,0:T(2,128)(2,1)}, u32[]{:S(2)}) copy-start(bf16[1,2,1024]{2,1,0:T(2,128)(2,1)} %param.17) | copy-start | bytes 12292
  3.7 7.9 %copy-start.6 = (s32[16]{0:T(128)S(1)}, s32[16]{0:T(128)}, u32[]{:S(2)}) copy-start(s32[16]{0:T(128)} %param.19) | copy-start | bytes 196
  3.7 10.5 %copy-start.7 = (s32[16]{0:T(128)S(1)}, s32[16]{0:T(128)}, u32[]{:S(2)}) copy-start(s32[16]{0:T(128)} %param.18) | copy-start | bytes 196
  3.7 12.9 %copy-start.5 = (s32[3]{0:T(128)S(1)}, s32[3]{0:T(128)}, u32[]{:S(2)}) copy-start(s32[3]{0:T(128)} %constant.107.clone.1) | copy-start | bytes 40
  9.0 5.7 %collective-permute-start.1 = (bf16[2,1,8192]{2,0,1:T(2,128)(2,1)S(1)}, bf16[2,1,8192]{2,0,1:T(2,128)(2,1)S(1)}, u32[]{:S(2)}, u32[]{:S(2)}) collective-permute-start(bf16[2,1,8192]{2,0,1:T(2,128)(2,1)S(1)} %get-tuple-element.161), channel_id=1, source_target_pairs={{0,2},{1,3},{2,0},{3,1},{4,6},{5,7},{6,4},{7,5},{8,10},{9,11},{10,... | collective-permute-start | bytes 98312 | tf_op jit(solution)/shard_map/ppermute | solution.py:22
  15.0 4.3 %collective-permute-start.2 = (bf16[4,1,8192]{2,0,1:T(4,128)(2,1)S(1)}, bf16[4,1,8192]{2,0,1:T(4,128)(2,1)S(1)}, u32[]{:S(2)}, u32[]{:S(2)}) collective-permute-start(bf16[4,1,8192]{2,0,1:T(4,128)(2,1)S(1)} %reshape.267), channel_id=1, source_target_pairs={{0,4},{1,5},{2,6},{3,7},{4,0},{5,1},{6,2},{7,3},{8,12},{9,13},{10,... | collective-permute-start | bytes 196616 | tf_op jit(solution)/shard_map/ppermute | solution.py:22
  19.5 14.0 %collective-permute-start.3 = (bf16[8,1,8192]{2,0,1:T(8,128)(2,1)S(1)}, bf16[8,1,8192]{2,0,1:T(8,128)(2,1)S(1)}, u32[]{:S(2)}, u32[]{:S(2)}) collective-permute-start(bf16[8,1,8192]{2,0,1:T(8,128)(2,1)S(1)} %reshape.268), channel_id=1, source_target_pairs={{0,8},{1,9},{2,10},{3,11},{4,12},{5,13},{6,14},{7,15},{8,0},{9,1},... | collective-permute-start | bytes 393224 | tf_op jit(solution)/shard_map/ppermute | solution.py:22
  30.9 1.9 %copy-start.4 = (s32[4]{0:T(128)S(1)}, s32[4]{0:T(128)}, u32[]{:S(2)}) copy-start(s32[4]{0:T(128)} %constant.112.clone.1) | copy-start | bytes 52
  62.6 7.8 %copy-start.1 = (f32[8,128,128]{2,1,0:T(8,128)S(1)}, f32[8,128,128]{2,1,0:T(8,128)}, u32[]{:S(2)}) copy-start(f32[8,128,128]{2,1,0:T(8,128)} %get-tuple-element.82) | copy-start | bytes 1572868
  65.3 10.6 %all-to-all-start = ((f32[16,1,64]{2,1,0:T(1,128)}), f32[16,1,64]{2,1,0:T(1,128)S(1)}, u32[]{:S(2)}, u32[]{:S(2)}) async-start(f32[16,1,64]{2,1,0:T(1,128)} %copy.86), calls=%async_computation | async-start | bytes 16384 | tf_op jit(solution)/shard_map/all_to_all | solution.py:185
  75.9 16.0 %all-to-all-start.1 = ((bf16[16,2,4096]{2,1,0:T(2,128)(2,1)}), bf16[16,2,4096]{2,1,0:T(2,128)(2,1)S(1)}, u32[]{:S(2)}, u32[]{:S(2)}) async-start(bf16[16,2,4096]{2,1,0:T(2,128)(2,1)} %reshape.331), calls=%async_computation.1 | async-start | bytes 524288 | tf_op jit(solution)/shard_map/all_to_all | solution.py:178
